TPU v7x, 32 devices: a whole 2x2x4 slice. The times are simulated.
32 devices in a mesh: dp: 16 (over z, y, core), owner: 2 (over x).
Axes of the slice: x: 2, y: 2, z: 4, core: 2. Of those that a mesh axis runs over, the one named last changes fastest.
Arguments:
- hidden: bfloat16 [2048, 4096], P('dp'), may hold values from -6 to 6
- norm_gain: float32 [4096], replicated, may hold values from 0.3 to 3
- cotangent: bfloat16 [2048, 6144], P('dp'), may hold values from -30 to 30
Outputs:
- update: bfloat16 [6144, 4096], P('dp', 'owner')
All inputs are finite; a program needn't handle non-finite values. Where the computation divides by a largest or mean magnitude, that divisor is 1e-20 or more.
Results may differ from a plain program's by a relative error of at most 0.014.
Values may be sent and summed in bfloat16 or wider, within the bound.
A program may use at most 128 MiB of HBM per device.

v0:
```python
import jax
import jax.numpy as jnp
from jax import lax
from jax.sharding import PartitionSpec as P

TILE = 1024


DAMPING = 0.1


def shards(hidden, norm_gain, cotangent):
    owners = lax.axis_size("owner")
    position = lax.axis_index("owner")
    groups = lax.axis_size("dp")
    tokens_here = hidden.shape[0]
    width = hidden.shape[1]
    out_width = cotangent.shape[1]
    blocks_all = (width + out_width) // TILE
    slots = (blocks_all + owners - 1) // owners
    states = hidden.astype(jnp.float32)
    normed = (
        states * lax.rsqrt(jnp.mean(states * states, axis=1, keepdims=True) + 1e-05) * norm_gain
    ).astype(jnp.bfloat16)
    source = jnp.concatenate([normed, cotangent], axis=1)
    columns = []
    for slot in range(slots):
        block = jnp.minimum(position + slot * owners, blocks_all - 1)
        columns.append(lax.dynamic_slice_in_dim(source, block * TILE, TILE, 1))
    pieces = jnp.stack(columns)
    partial_value = jnp.einsum("stk,stl->skl", pieces, pieces, preferred_element_type=jnp.float32)
    identity = jnp.eye(TILE, dtype=jnp.float32)
    factor = lax.psum(partial_value, "dp")
    matrix = factor / (tokens_here * groups) + DAMPING * identity
    scale = 1.0 / jnp.max(jnp.sum(jnp.abs(matrix), axis=2), axis=1)
    first = 2.0 * scale[:, None, None] * identity - (scale * scale)[:, None, None] * matrix
    first_low = first.astype(jnp.bfloat16)
    matrix_low = matrix.astype(jnp.bfloat16)
    product = jnp.einsum(
        "skl,slm->skm", first_low, matrix_low, preferred_element_type=jnp.float32
    ).astype(jnp.bfloat16)
    inverse = (
        2.0 * first
        - jnp.einsum("skl,slm->skm", product, first_low, preferred_element_type=jnp.float32)
    ).astype(jnp.bfloat16)
    precond = jnp.einsum(
        "stk,skl->stl", pieces, inverse, preferred_element_type=jnp.float32
    ).astype(jnp.bfloat16)
    gathered = lax.all_gather(precond[:, None], "owner", axis=1, tiled=True)
    ordered = gathered.reshape(slots * owners, tokens_here, TILE)[:blocks_all]
    inputs_side = width // TILE
    pre_in = jnp.transpose(ordered[:inputs_side], (1, 0, 2)).reshape(tokens_here, width)
    pre_out = jnp.transpose(ordered[inputs_side:], (1, 0, 2)).reshape(tokens_here, out_width)
    own_rows = width // owners
    mine_in = lax.dynamic_slice_in_dim(pre_in, position * own_rows, own_rows, 1)
    summed = lax.psum_scatter(
        jnp.einsum("tk,tl->kl", pre_out, mine_in, preferred_element_type=jnp.float32).astype(
            jnp.bfloat16
        ),
        "dp",
        scatter_dimension=0,
        tiled=True,
    ).astype(jnp.float32)
    squares = lax.psum(jnp.sum(summed * summed), ("dp", "owner"))
    return (summed * lax.rsqrt(squares / (width * out_width) + 1e-06)).astype(jnp.bfloat16)


def solution(mesh):
    in_specs = (P("dp", None), P(), P("dp", None))
    out_specs = P("dp", "owner")
    return jax.shard_map(shards, mesh=mesh, in_specs=in_specs, out_specs=out_specs, check_vma=False)
```

profile of v0, /device:TPU:0, one launch (start us, length us, event | category | flops | bytes accessed | tf_op | source)
XLA Modules:
  0.0 812.2 jit_solution(15616103901060733694)
XLA Ops:
  6.5 1.6 fusion.17
  8.2 1.6 fusion.19
  9.8 0.9 bitcast_dynamic-update-slice_fusion.4
  10.6 0.8 bitcast_dynamic-update-slice_fusion.3
  11.5 0.8 bitcast_dynamic-update-slice_fusion.2
  12.3 0.8 bitcast_dynamic-update-slice_fusion.1
  13.1 0.8 bitcast_dynamic-update-slice_fusion
  14.0 11.8 %fusion.36 = f32[5,1024,1024]{2,1,0:T(8,128)} fusion(bf16[5,128,1024]{2,1,0:T(8,128)(2,1)} %bitcast_dynamic-update-slice_fusion), kind=kOutput, calls=%fused_computation.54 | convolution fusion | flops 1342177280 | bytes 22282240 | tf_op jit(solution)/shard_map/stk,stl->skl/dot_general | solution.py:31
  26.0 2.4 fusion.14
  28.5 2.5 fusion.13
  30.9 359.7 %all-reduce.2.cloned.1.call-done = f32[5,1024,1024]{2,1,0:T(8,128)} async-done(((f32[5,1024,1024]{2,1,0:T(8,128)}), f32[5,1024,1024]{2,1,0:T(8,128)}) %all-reduce.2.cloned.1.call-update) | async-done | bytes 20971536 | tf_op jit(solution)/shard_map/psum | solution.py:33
  390.7 9.1 %abs_reduce_fusion = f32[5,1024]{1,0:T(8,128)S(1)} fusion(f32[5,1024,1024]{2,1,0:T(8,128)} %all-reduce.2.cloned.1.call-done, f32[1024,1024]{1,0:T(8,128)} %fusion.14), kind=kLoop, calls=%fused_computation.3 | loop fusion | flops 20966400 | bytes 25186304 | tf_op jit(solution)/shard_map/reduce_sum | solution.py:35
  399.9 29.7 %fusion.2 = bf16[5,1024,1024]{2,1,0:T(8,128)(2,1)} fusion(f32[5,1024,1024]{2,1,0:T(8,128)} %all-reduce.2.cloned.1.call-done, f32[1024,1024]{1,0:T(8,128)} %fusion.14, f32[5]{0:T(128)S(1)} %mul.110, f32[1024,1024]{1,0:T(8,128)} %fusion.13, f32[5]{0:T(128)S(1)} %get-tuple-element.5), kind=kOutput, calls=%fused_computation.7 | convolution fusion | flops 10784604160 | bytes 39845928 | tf_op jit(solution)/shard_map/skl,slm->skm/dot_general | solution.py:39
  429.7 29.7 %fusion.20 = bf16[5,128,1024]{2,1,0:T(8,128)(2,1)} fusion(bf16[5,128,1024]{2,1,0:T(8,128)(2,1)} %bitcast_dynamic-update-slice_fusion, f32[5,1024,1024]{2,1,0:T(8,128)} %all-reduce.2.cloned.1.call-done, f32[5]{0:T(128)S(1)} %mul.110, f32[1024,1024]{1,0:T(8,128)} %fusion.13, f32[5]{0:T(128)S(1)} %get-tuple-element.5, f32[1024,1024]{1,0:T(8,128)} %fusion.14, ...), kind=kOutput, calls=%fused_computation.35 | convolution fusion | flops 12153651200 | bytes 42467368 | tf_op jit(solution)/shard_map/stk,skl->stl/dot_general | solution.py:46
  459.7 38.7 %all-gather.3.cloned.1.call-done = bf16[5,256,1024]{2,1,0:T(8,128)(2,1)} async-done(((bf16[5,128,1024]{2,1,0:T(8,128)(2,1)}), bf16[5,256,1024]{2,1,0:T(8,128)(2,1)}) %all-gather.3.cloned.1.call-update) | async-done | bytes 2621456 | tf_op jit(solution)/shard_map/all_gather | solution.py:49
  498.4 1.4 slice-done
  499.8 0.9 copy.9
  500.7 1.3 slice.19
  502.0 1.3 copy.10
  503.3 12.7 %convolution_convert_fusion = bf16[6144,2048]{1,0:T(8,128)(2,1)} fusion(bf16[128,6144]{0,1:T(8,128)(2,1)S(1)} %bitcast.23, bf16[128,4096]{0,1:T(8,128)(2,1)} %bitcast.26, s32[]{:T(128)S(6)} %select_n.23), kind=kOutput, calls=%fused_computation | convolution fusion | flops 3233808384 | bytes 27262980 | tf_op jit(solution)/shard_map/tk,tl->kl/dot_general | solution.py:57
  516.1 243.7 %reduce-scatter.2.cloned.1.call-done = bf16[384,2048]{1,0:T(8,128)(2,1)} async-done(((bf16[6144,2048]{1,0:T(8,128)(2,1)}), bf16[384,2048]{1,0:T(8,128)(2,1)}) %reduce-scatter.2.cloned.1.call-update) | async-done | bytes 1572880 | tf_op jit(solution)/shard_map/reduce_scatter | solution.py:56
  759.7 2.8 fusion.15
  762.6 39.5 %psum.15 = f32[]{:T(128)} all-reduce(f32[]{:T(128)} %fusion.15), channel_id=1, replica_groups=mesh['dp'=16,'owner'=2] {'dp','owner'}, use_global_device_ids=true, to_apply=%region_6.0 | all-reduce | flops 1 | bytes 8 | tf_op jit(solution)/shard_map/psum | solution.py:64
  802.7 2.9 fusion.16
  (13 shorter events, 0.7 us)
Async XLA Ops:
  6.5 3.2 copy-start
  6.5 384.1 %all-reduce.2.cloned.1.call-start = ((), (), s32[]{:S(2)}) async-start(), calls=%async_computation.1 | async-start | bytes 41943040 | tf_op jit(solution)/shard_map/psum | solution.py:33
  25.8 472.6 %all-gather.3.cloned.1.call-start = ((), (), s32[]{:S(2)}) async-start(), calls=%async_computation.3 | async-start | bytes 3932160 | tf_op jit(solution)/shard_map/all_gather | solution.py:49
  459.4 300.3 %reduce-scatter.2.cloned.1.call-start = ((), (), s32[]{:S(2)}) async-start(), calls=%async_computation.2 | async-start | bytes 26738688 | tf_op jit(solution)/shard_map/reduce_scatter | solution.py:56
  498.4 1.4 slice-start
Sparse Core Ops, SparseCore 0:
  25.9 364.6 all-reduce.1
  459.5 38.8 all-gather.2
  516.2 243.5 reduce-scatter.1
where the time goes:
time: 813 us; the launch traced here: 812 us
  waiting for transfers between devices  642 us (79%)
  matrix products  83.9 us (10%)
  blocking collectives  39.5 us (5%)
  other arithmetic  27.3 us (3%)
  between operations  13.8 us (2%)
    psum x1, waiting for transfers between devices, shards(): factor = lax.psum(partial_value, 'dp')  360 us
    reduce_scatter x1, waiting for transfers between devices, shards(): lax.psum_scatter(jnp.einsum('tk,tl->kl', pre_out, mine_in, preferred_elem...  244 us
    psum x1, blocking collectives, shards(): squares = lax.psum(jnp.sum(summed * summed), ('dp', 'owner'))  39.5 us
    all_gather x1, waiting for transfers between devices, shards(): gathered = lax.all_gather(precond[:, None], 'owner', axis=1, tiled=True)  38.7 us
    dot_general x1, matrix products, shards(): jnp.einsum('skl,slm->skm', first_low, matrix_low, preferred_element_type=...  29.7 us
    dot_general x1, matrix products, shards(): jnp.einsum('stk,skl->stl', pieces, inverse, preferred_element_type=jnp.fl...  29.7 us
  transfers between devices with their start and end apart: 3, of which 3 were waited for; matrix products, arithmetic and copies ran while one was open for 1% of the time, Pallas kernels for 0%

commit v1 on v0

v1 whole, which is shorter than its diff:
```python
import jax
import jax.numpy as jnp
from jax import lax
from jax.sharding import PartitionSpec as P

TILE = 1024


DAMPING = 0.1


def contract(left, right, left_dim, right_dim):
    return lax.dot_general(
        left, right, (((left_dim,), (right_dim,)), ((), ())), preferred_element_type=jnp.float32
    )


def inverse_of(piece, tokens):
    identity = jnp.eye(TILE, dtype=jnp.float32)
    matrix = contract(piece, piece, 0, 0) / tokens + DAMPING * identity
    scale = 1.0 / jnp.max(jnp.sum(jnp.abs(matrix), axis=1))
    first = 2.0 * scale * identity - (scale * scale) * matrix
    first_low = first.astype(jnp.bfloat16)
    matrix_low = matrix.astype(jnp.bfloat16)
    product = contract(first_low, matrix_low, 1, 0).astype(jnp.bfloat16)
    return (2.0 * first - contract(product, first_low, 1, 0)).astype(jnp.bfloat16)


def shards(hidden, norm_gain, cotangent):
    owners = lax.axis_size("owner")
    position = lax.axis_index("owner")
    groups = lax.axis_size("dp")
    group = lax.axis_index("dp")
    tokens_here = hidden.shape[0]
    tokens = tokens_here * groups
    width = hidden.shape[1]
    out_width = cotangent.shape[1]
    strip = out_width // groups
    own = width // owners
    in_width = max(own, TILE)

    firsts = jnp.array([(g * strip) // TILE for g in range(groups)], jnp.int32)
    lasts = jnp.array([((g + 1) * strip - 1) // TILE for g in range(groups)], jnp.int32)
    odd = lax.rem(position, 2) == 1
    wanted = jnp.where(odd, lasts, firsts)
    outgoing = jnp.stack(
        [
            lax.dynamic_slice_in_dim(cotangent, wanted[g] * TILE, TILE, 1)
            for g in range(groups)
        ]
    )
    out_piece = lax.all_to_all(outgoing, "dp", 0, 0, tiled=True).reshape(tokens, TILE)

    states = hidden.astype(jnp.float32)
    normed = (
        states * lax.rsqrt(jnp.mean(states * states, axis=1, keepdims=True) + 1e-05) * norm_gain
    ).astype(jnp.bfloat16)
    in_start = (position * own) // TILE * TILE
    mine = lax.dynamic_slice_in_dim(normed, in_start, in_width, 1)
    in_piece = lax.all_gather(mine, "dp", axis=0, tiled=True)

    out_inverse = inverse_of(out_piece, tokens)
    padded = jnp.pad(out_inverse, ((0, 0), (strip, strip)))
    offset = group * strip - wanted[group] * TILE
    strip_inverse = lax.dynamic_slice_in_dim(padded, offset + strip, strip, 1)
    part = contract(out_piece, strip_inverse, 1, 0).astype(jnp.bfloat16)
    other = lax.ppermute(part, "owner", [(o, o ^ 1) for o in range(owners)])
    column_block = (group * strip + jnp.arange(strip, dtype=jnp.int32)) // TILE
    pre_out = jnp.where((column_block == wanted[group])[None, :], part, other)

    results = []
    for block in range(in_width // TILE):
        piece = in_piece[:, block * TILE : (block + 1) * TILE]
        inverse = inverse_of(piece, tokens)
        if own < TILE:
            inverse = lax.dynamic_slice_in_dim(inverse, position * own - in_start, own, 1)
        cross = contract(pre_out, piece, 0, 0).astype(jnp.bfloat16)
        results.append(contract(cross, inverse, 1, 0))
    summed = jnp.concatenate(results, axis=1)
    squares = lax.psum(jnp.sum(summed * summed), ("dp", "owner"))
    return (summed * lax.rsqrt(squares / (width * out_width) + 1e-06)).astype(jnp.bfloat16)


def solution(mesh):
    in_specs = (P("dp", None), P(), P("dp", None))
    out_specs = P("dp", "owner")
    return jax.shard_map(shards, mesh=mesh, in_specs=in_specs, out_specs=out_specs, check_vma=False)
```

time: 813 us -> 328 us (0.40)
  waiting for transfers between devices: 642 us -> 91.5 us
  local copies, waits for them, and re-layouts: 4.9 us -> 43.5 us
  other arithmetic: 27.3 us -> 11.9 us
  blocking collectives: 39.5 us -> 54.5 us
  between operations: 13.8 us -> 27.3 us
  starting transfers between devices: 0.49 us -> 9.01 us
    psum x1 -> x0, waiting for transfers between devices: 360 us -> none  [shards(): factor = lax.psum(partial_value, 'dp')]
    reduce_scatter x1 -> x0, waiting for transfers between devices: 244 us -> none  [shards(): lax.psum_scatter(jnp.einsum('tk,tl->kl', pre_out, mine_in, preferred_elem...]
    all_to_all x0 -> x1, waiting for transfers between devices: none -> 91.5 us  [shards(): lax.all_to_all(outgoing, 'dp', 0, 0, tiled=True).reshape(tokens, TILE)]
    all_gather x1, waiting for transfers between devices: 38.7 us -> 0.01 us  [shards(): in_piece = lax.all_gather(mine, 'dp', axis=0, tiled=True)]
    dynamic_slice x0 -> x19, local copies, waits for them, and re-layouts: none -> 19.5 us  [the longest x17 18.8 us: shards(): lax.dynamic_slice_in_dim(cotangent, wanted[g] * TILE, TILE, 1)]
    unnamed x2 -> x35, local copies, waits for them, and re-layouts: 0.01 us -> 16.7 us
    psum x1, blocking collectives: 39.5 us -> 54.5 us  [shards(): squares = lax.psum(jnp.sum(summed * summed), ('dp', 'owner'))]
    reduce_sum x1 -> x0, other arithmetic: 9.14 us -> none  [shards(): scale = 1.0 / jnp.max(jnp.sum(jnp.abs(matrix), axis=2), axis=1)]
  transfers between devices with their start and end apart: 3 -> 3, of which waited for: 3 -> 1; matrix products, arithmetic and copies ran while one was open for 1% -> 37% of each run, Pallas kernels for 0% -> 0%
where the time goes in v1:
time: 328 us; the launch traced here: 322 us
  waiting for transfers between devices  91.5 us (28%)
  matrix products  84.1 us (26%)
  blocking collectives  54.5 us (17%)
  local copies, waits for them, and re-layouts  43.5 us (13%)
  between operations  27.3 us (8%)
  other arithmetic  11.9 us (4%)
  starting transfers between devices  9.01 us (3%)
    all_to_all x1, waiting for transfers between devices, shards(): lax.all_to_all(outgoing, 'dp', 0, 0, tiled=True).reshape(tokens, TILE)  91.5 us
    dot_general x9, matrix products, contract(): lax.dot_general(left, right, (((left_dim,), (right_dim,)), ((), ())), pre...  84.1 us
    psum x1, blocking collectives, shards(): squares = lax.psum(jnp.sum(summed * summed), ('dp', 'owner'))  54.5 us
    dynamic_slice x17, local copies, waits for them, and re-layouts, shards(): lax.dynamic_slice_in_dim(cotangent, wanted[g] * TILE, TILE, 1)  18.8 us
    unnamed x35, local copies, waits for them, and re-layouts  16.7 us
    all_to_all x1, starting transfers between devices, shards(): lax.all_to_all(outgoing, 'dp', 0, 0, tiled=True).reshape(tokens, TILE)  7.47 us
    all_to_all x1, local copies, waits for them, and re-layouts, shards(): lax.all_to_all(outgoing, 'dp', 0, 0, tiled=True).reshape(tokens, TILE)  6.56 us
  transfers between devices with their start and end apart: 3, of which 1 were waited for; matrix products, arithmetic and copies ran while one was open for 37% of the time, Pallas kernels for 0%

profile of v1, /device:TPU:0, one launch (start us, length us, event | category | flops | bytes accessed | tf_op | source)
XLA Modules:
  0.0 321.7 jit_solution(2514432359440347336)
XLA Ops:
  6.6 2.9 convert_element_type.64
  11.1 2.2 fusion.96
  25.7 1.8 copy.23
  27.6 1.8 copy.24
  29.4 1.8 copy.25
  31.2 1.8 copy.26
  33.0 1.8 copy.27
  34.8 1.8 copy.28
  36.6 1.8 copy.29
  38.4 1.8 copy.30
  49.7 1.7 bitcast_dynamic-update-slice_fusion.11
  60.3 7.5 %all-to-all-start = ((bf16[16,128,1024]{1,2,0:T(8,128)(2,1)}), bf16[16,128,1024]{1,2,0:T(8,128)(2,1)}, u32[]{:S(2)}, u32[]{:S(2)}) async-start(bf16[16,128,1024]{1,2,0:T(8,128)(2,1)} %bitcast_dynamic-update-slice_fusion), calls=%async_computation | async-start | bytes 8388608 | tf_op jit(solution)/shard_map/all_to_all | solution.py:52
  69.0 91.5 %all-to-all-done = bf16[16,128,1024]{1,2,0:T(8,128)(2,1)} async-done(((bf16[16,128,1024]{1,2,0:T(8,128)(2,1)}), bf16[16,128,1024]{1,2,0:T(8,128)(2,1)}, u32[]{:S(2)}, u32[]{:S(2)}) %all-to-all-start) | async-done | bytes 4194336 | tf_op jit(solution)/shard_map/all_to_all | solution.py:52
  160.5 9.9 %abs_reduce_fusion.2 = (f32[1024]{0:T(1024)S(1)}, f32[1024,1024]{0,1:T(8,128)}) fusion(bf16[16,128,1024]{1,2,0:T(8,128)(2,1)} %all-to-all-done), kind=kOutput, calls=%fused_computation.12 | convolution fusion | flops 4301257728 | bytes 8392704 | tf_op jit(solution)/shard_map/dot_general | solution.py:13
  171.7 6.6 %copy.39 = bf16[16,128,1024]{2,1,0:T(8,128)(2,1)} copy(bf16[16,128,1024]{1,2,0:T(8,128)(2,1)} %all-to-all-done) | data formatting | bytes 8388608 | tf_op jit(solution)/shard_map/all_to_all | solution.py:52
  178.2 11.9 %subtract_convert_fusion.2 = bf16[1024,1024]{0,1:T(8,128)(2,1)} fusion(f32[1024,1024]{0,1:T(8,128)} %get-tuple-element.41, f32[]{:T(128)S(6)} %mul.246, f32[]{:T(128)S(6)} %mul.243), kind=kOutput, calls=%fused_computation.10 | convolution fusion | flops 4314890240 | bytes 6291464 | tf_op jit(solution)/shard_map/dot_general | solution.py:13
  190.1 4.8 %convolution_convert_fusion = bf16[2048,384]{1,0:T(8,128)(2,1)S(1)} fusion(bf16[2048,1024]{1,0:T(8,128)(2,1)} %bitcast.59, s32[]{:T(128)S(6)} %select_n.104, bf16[1024,1024]{0,1:T(8,128)(2,1)} %subtract_convert_fusion.2), kind=kOutput, calls=%fused_computation.29 | convolution fusion | flops 1611399168 | bytes 7864324 | tf_op jit(solution)/shard_map/dot_general | solution.py:13
  196.4 10.1 %abs_reduce_fusion.1 = (f32[1024]{0:T(1024)S(1)}, f32[1024,1024]{0,1:T(8,128)}) fusion(bf16[2048,2048]{1,0:T(8,128)(2,1)} %all-gather.2.cloned.1.call-done), kind=kOutput, calls=%fused_computation.9 | convolution fusion | flops 4301257728 | bytes 8392704 | tf_op jit(solution)/shard_map/dot_general | solution.py:13
  207.8 10.3 %abs_reduce_fusion = (f32[1024]{0:T(1024)S(1)}, f32[1024,1024]{0,1:T(8,128)}) fusion(bf16[2048,2048]{1,0:T(8,128)(2,1)} %all-gather.2.cloned.1.call-done), kind=kOutput, calls=%fused_computation.6 | convolution fusion | flops 4301257728 | bytes 8392704 | tf_op jit(solution)/shard_map/dot_general | solution.py:13
  219.4 12.3 %subtract_convert_fusion.1 = bf16[1024,1024]{0,1:T(8,128)(2,1)} fusion(f32[]{:T(128)S(6)} %mul.261, f32[1024,1024]{0,1:T(8,128)} %get-tuple-element.43, f32[]{:T(128)S(6)} %mul.258), kind=kOutput, calls=%fused_computation.7 | convolution fusion | flops 4328521728 | bytes 6291464 | tf_op jit(solution)/shard_map/dot_general | solution.py:13
  231.7 12.4 %subtract_convert_fusion = bf16[1024,1024]{0,1:T(8,128)(2,1)} fusion(f32[]{:T(128)S(6)} %mul.268, f32[1024,1024]{0,1:T(8,128)} %get-tuple-element.39, f32[]{:T(128)S(6)} %mul.265), kind=kOutput, calls=%fused_computation.4 | convolution fusion | flops 4328521728 | bytes 6291464 | tf_op jit(solution)/shard_map/dot_general | solution.py:13
  244.1 6.0 %fusion.101 = f32[384,1024]{1,0:T(8,128)S(1)} fusion(bf16[1024,1024]{0,1:T(8,128)(2,1)} %subtract_convert_fusion.1, bf16[2048,2048]{1,0:T(8,128)(2,1)} %all-gather.2.cloned.1.call-done, bf16[2048,384]{1,0:T(8,128)(2,1)S(1)} %convolution_convert_fusion, bf16[2048,384]{1,0:T(8,128)(2,1)} %collective-permute-done, pred[384]{0:T(512)(128)(4,1)S(1)} %fusion.105), kind=kOutput, calls=%fused_computation.60 | convolution fusion | flops 2417098752 | bytes 11010432 | tf_op jit(solution)/shard_map/dot_general | solution.py:13
  250.1 6.4 %fusion.98 = f32[384,1024]{1,0:T(8,128)S(1)} fusion(bf16[1024,1024]{0,1:T(8,128)(2,1)} %subtract_convert_fusion, bf16[2048,2048]{1,0:T(8,128)(2,1)} %all-gather.2.cloned.1.call-done, bf16[2048,384]{1,0:T(8,128)(2,1)} %copy-done.9, bf16[2048,384]{1,0:T(8,128)(2,1)} %collective-permute-done, pred[384]{0:T(512)(128)(4,1)S(1)} %fusion.105), kind=kOutput, calls=%fused_computation.59 | convolution fusion | flops 2417098752 | bytes 11010432 | tf_op jit(solution)/shard_map/dot_general | solution.py:13
  257.8 54.5 %psum.7 = f32[]{:T(128)} all-reduce(f32[]{:T(128)} %multiply_reduce_fusion), channel_id=1, replica_groups=mesh['dp'=16,'owner'=2] {'dp','owner'}, use_global_device_ids=true, to_apply=%region_8.9 | all-reduce | flops 1 | bytes 8 | tf_op jit(solution)/shard_map/psum | solution.py:80
  (60 shorter events, 29.0 us)
Async XLA Ops:
  6.5 6.8 %copy-start.7 = (s32[16]{0:T(128)S(1)}, s32[16]{0:T(128)}, u32[]{:S(2)}) copy-start(s32[16]{0:T(128)} %constant.105.clone) | copy-start | bytes 196
  6.5 6.8 %copy-start.8 = (s32[16]{0:T(128)S(1)}, s32[16]{0:T(128)}, u32[]{:S(2)}) copy-start(s32[16]{0:T(128)} %constant.106.clone) | copy-start | bytes 196
  6.5 4.5 %copy-start.6 = (f32[4096]{0:T(1024)S(1)}, f32[4096]{0:T(1024)}, u32[]{:S(2)}) copy-start(f32[4096]{0:T(1024)} %param.6) | copy-start | bytes 49156
  6.5 17.6 %copy-start = (bf16[128,6144]{1,0:T(8,128)(2,1)S(1)}, bf16[128,6144]{1,0:T(8,128)(2,1)}, u32[]{:S(2)}) copy-start(bf16[128,6144]{1,0:T(8,128)(2,1)} %param.7) | copy-start | bytes 4718596
  6.5 189.9 %all-gather.2.cloned.1.call-start = ((), (), s32[]{:S(2)}) async-start(), calls=%async_computation.1 | async-start | bytes 8912896 | tf_op jit(solution)/shard_map/all_gather | solution.py:60
  25.7 14.5 %copy-start.1 = (bf16[128,1024]{1,0:T(8,128)(2,1)S(1)}, bf16[128,1024]{1,0:T(8,128)(2,1)}, u32[]{:S(2)}) copy-start(bf16[128,1024]{1,0:T(8,128)(2,1)} %get-tuple-element.11) | copy-start | bytes 786436
  41.9 13.4 %copy-start.2 = (bf16[128,1024]{0,1:T(8,128)(2,1)S(1)}, bf16[128,1024]{0,1:T(8,128)(2,1)}, u32[]{:S(2)}) copy-start(bf16[128,1024]{0,1:T(8,128)(2,1)} %copy.32) | copy-start | bytes 786436
  42.1 12.5 %copy-start.3 = (bf16[128,1024]{0,1:T(8,128)(2,1)S(1)}, bf16[128,1024]{0,1:T(8,128)(2,1)}, u32[]{:S(2)}) copy-start(bf16[128,1024]{0,1:T(8,128)(2,1)} %copy.31) | copy-start | bytes 786436
  42.3 11.5 %copy-start.4 = (bf16[128,1024]{0,1:T(8,128)(2,1)S(1)}, bf16[128,1024]{0,1:T(8,128)(2,1)}, u32[]{:S(2)}) copy-start(bf16[128,1024]{0,1:T(8,128)(2,1)} %copy.30) | copy-start | bytes 786436
  42.4 10.7 %copy-start.5 = (bf16[128,1024]{0,1:T(8,128)(2,1)S(1)}, bf16[128,1024]{0,1:T(8,128)(2,1)}, u32[]{:S(2)}) copy-start(bf16[128,1024]{0,1:T(8,128)(2,1)} %copy.29) | copy-start | bytes 786436
  60.3 100.1 %all-to-all-start = ((bf16[16,128,1024]{1,2,0:T(8,128)(2,1)}), bf16[16,128,1024]{1,2,0:T(8,128)(2,1)}, u32[]{:S(2)}, u32[]{:S(2)}) async-start(bf16[16,128,1024]{1,2,0:T(8,128)(2,1)} %bitcast_dynamic-update-slice_fusion), calls=%async_computation | async-start | bytes 8388608 | tf_op jit(solution)/shard_map/all_to_all | solution.py:52
  194.9 49.2 %copy-start.9 = (bf16[2048,384]{1,0:T(8,128)(2,1)}, bf16[2048,384]{1,0:T(8,128)(2,1)S(1)}, u32[]{:S(2)}) copy-start(bf16[2048,384]{1,0:T(8,128)(2,1)S(1)} %convolution_convert_fusion) | copy-start | bytes 4718596
  194.9 49.2 %collective-permute-start = (bf16[2048,384]{1,0:T(8,128)(2,1)S(1)}, bf16[2048,384]{1,0:T(8,128)(2,1)}, u32[]{:S(2)}, u32[]{:S(2)}) collective-permute-start(bf16[2048,384]{1,0:T(8,128)(2,1)S(1)} %convolution_convert_fusion), channel_id=1, source_target_pairs={{0,1},{1,0},{2,3},{3,2},{4,5},{5,4},{6,7},{7,6},{8,9},{9,8},{10,11... | collective-permute-start | bytes 4718600 | tf_op jit(solution)/shard_map/ppermute | solution.py:67
Sparse Core Ops, SparseCore 0:
  13.4 105.0 all-gather.1
